TPU v7x, 1024 devices: a whole 4x4x32 slice. The times are simulated.
1024 devices in a mesh: chan: 32 (over y, z_lo), ctx: 32 (over z_hi, x, core).
Axes of the slice: x: 4, y: 4, z: 32 (z_hi: 4, z_lo: 8; z = z_hi * 8 + z_lo), core: 2. Of those that a mesh axis runs over, the one named last changes fastest.
Arguments:
- key_proj: bfloat16 [32768, 4096], P('ctx', 'chan'), may hold values from -6 to 6
- value_proj: bfloat16 [32768, 4096], P('ctx', 'chan'), may hold values from -6 to 6
- query_proj: bfloat16 [32768, 4096], P('ctx', 'chan'), may hold values from -6 to 6
- short_filter: bfloat16 [3, 3, 4096], P(None, None, 'chan'), may hold values from -3.5 to 3.5
- decay_rate: float32 [16, 4096], P(None, 'chan'), may hold values from 1.5258789e-05 to 0.05
- residue: float32 [16, 4096], P(None, 'chan'), may hold values from -0.03 to 0.03
- skip_gain: float32 [4096], P('chan'), may hold values from -1 to 1
- out_weight: bfloat16 [4096, 4096], P('chan'), may hold values from -0.1875 to 0.1875
Outputs:
- block_out: bfloat16 [32768, 4096], P('ctx', 'chan')
All inputs are finite; a program needn't handle non-finite values.
Results may differ from a plain program's by a relative error of at most 0.023.
Values may be sent and summed in bfloat16 or wider, within the bound.
No kernel may reach another device: no remote copies, remote signals or barrier semaphores. Data moves between devices by JAX's collectives and lax.ppermute only.
A program may use at most 64 MiB of HBM per device.

v0:
```python
import jax
import jax.numpy as jnp
from jax import lax
from jax.sharding import PartitionSpec as P


def passed_along(value, axis, steps):
    count = lax.axis_size(axis)
    initial, last = (max(0, -steps), min(count, count - steps))
    return lax.ppermute(value, axis, [(source, source + steps) for source in range(initial, last)])


def modal_conv(signal, decay_rate, residue):
    channels, length = signal.shape
    tile_rows = 128
    blocks = length // tile_rows
    rates = decay_rate.T
    weights = residue.T
    position = jnp.arange(tile_rows).astype(jnp.float32)
    kernel = jnp.einsum(
        "cm,cml->cl",
        weights,
        jnp.exp(-rates[:, :, None] * position[None, None, :]),
        precision=lax.Precision.HIGHEST,
    )
    lag_index = jnp.arange(tile_rows)[:, None] - jnp.arange(tile_rows)[None, :]
    toeplitz = jnp.where(
        lag_index[None] >= 0, kernel[:, jnp.clip(lag_index, 0, tile_rows - 1)], jnp.float32(0.0)
    )
    tiles = signal.reshape(channels, blocks, tile_rows)
    inside = jnp.einsum("cij,cnj->cni", toeplitz, tiles, precision=lax.Precision.HIGHEST)
    leaving = jnp.exp(-rates[:, :, None] * (tile_rows - position)[None, None, :])
    deposit = jnp.einsum("cmj,cnj->cnm", leaving, tiles, precision=lax.Precision.HIGHEST)
    factor = jnp.broadcast_to(jnp.exp(-rates * tile_rows)[:, None, :], deposit.shape)

    def combine(first, second):
        return (first[0] * second[0], first[1] * second[0] + second[1])

    _, ending = lax.associative_scan(combine, (factor, deposit), axis=1)
    starting = jnp.concatenate([jnp.zeros_like(ending[:, :1]), ending[:, :-1]], 1)
    arriving = weights[:, :, None] * jnp.exp(-rates[:, :, None] * position[None, None, :])
    carried = jnp.einsum("cnm,cmi->cni", starting, arriving, precision=lax.Precision.HIGHEST)
    return ((inside + carried).reshape(channels, length), ending[:, -1])


def local(
    key_proj, value_proj, query_proj, short_filter, decay_rate, residue, skip_gain, out_weight
):
    tap_count = short_filter.shape[1]
    row_count = key_proj.shape[0]
    stacked = jnp.stack([query_proj, key_proj, value_proj], 0)
    tail_rows = passed_along(stacked[:, row_count - (tap_count - 1) :], "ctx", 1)
    padded = jnp.concatenate([tail_rows, stacked], 1).astype(jnp.float32)
    taps = short_filter.astype(jnp.float32)
    feat = jnp.zeros(stacked.shape, jnp.float32)
    for tap_index in range(tap_count):
        offset = tap_count - 1 - tap_index
        feat = feat + taps[:, tap_index][:, None, :] * padded[:, offset : offset + row_count]
    product = (feat[1] * feat[2]).astype(jnp.bfloat16)
    columns = lax.all_to_all(product.T, "ctx", split_axis=0, concat_axis=1, tiled=True)
    share = columns.shape[0]
    offset_chan = lax.axis_index("ctx") * share
    rates = lax.dynamic_slice_in_dim(decay_rate, offset_chan, share, 1)
    weights = lax.dynamic_slice_in_dim(residue, offset_chan, share, 1)
    gains = lax.dynamic_slice_in_dim(skip_gain, offset_chan, share, 0)
    signal = columns.astype(jnp.float32)
    conv, _ = modal_conv(signal, rates, weights)
    answer = (conv + gains[:, None] * signal).astype(jnp.bfloat16)
    long_out = lax.all_to_all(answer, "ctx", split_axis=1, concat_axis=0, tiled=True).T
    gated = (feat[0] * long_out.astype(jnp.float32)).astype(jnp.bfloat16)
    columns = out_weight
    summed = lax.psum_scatter(
        lax.dot_general(
            columns, gated, (((0,), (1,)), ((), ())), preferred_element_type=jnp.float32
        ).astype(jnp.bfloat16),
        "chan",
        scatter_dimension=0,
        tiled=True,
    ).astype(jnp.float32)
    return summed.T.astype(jnp.bfloat16)


def solution(mesh):
    placed = (
        P("ctx", "chan"),
        P("ctx", "chan"),
        P("ctx", "chan"),
        P(None, None, "chan"),
        P(None, "chan"),
        P(None, "chan"),
        P("chan"),
        P("chan", None),
    )
    return jax.shard_map(
        local, mesh=mesh, in_specs=placed, out_specs=P("ctx", "chan"), check_vma=False
    )
```

profile of v0, /device:TPU:2, one launch (start us, length us, event | category | flops | bytes accessed | tf_op | source)
XLA Modules:
  0.0 573.6 jit_solution(7735071749771257761)
XLA Ops:
  10.0 1.9 collective-permute-start
  12.0 4.0 collective-permute-done
  18.5 44.7 %all-to-all-start = ((bf16[32,4,1024]{2,1,0:T(4,128)(2,1)}), bf16[32,4,1024]{2,1,0:T(4,128)(2,1)S(1)}, u32[]{:S(2)}, u32[]{:S(2)}) async-start(bf16[32,4,1024]{2,1,0:T(4,128)(2,1)} %all_to_all.20), calls=%async_computation | async-start | bytes 524288 | tf_op jit(solution)/shard_map/all_to_all | solution.py:60
  67.1 54.8 %gather_fusion = f32[16384,4]{1,0:T(8,128)} fusion(f32[4,128]{0,1:T(8,128)S(1)} %copy.135, s32[16384]{0:T(1024)S(1)} %fusion.13), kind=kCustom, calls=%fused_computation | custom fusion | bytes 589824 | tf_op jit(solution)/shard_map/gather | solution.py:28
  121.9 5.2 copy.127
  129.4 1.7 slice.261
  148.9 1.5 slice.233
  157.9 3.3 pad.53
  162.7 3.3 pad.52
  169.8 3.3 pad.54
  173.1 3.3 pad.55
  180.2 3.3 pad.56
  183.5 3.4 pad.57
  189.8 1.7 pad.58
  191.5 3.4 pad.59
  197.8 1.8 pad.61
  201.9 2.0 pad.63
  206.8 2.4 pad.121
  209.6 1.8 convolution_add_fusion
  213.7 55.6 %all_to_all.26 = bf16[4,32,1024]{2,0,1:T(4,128)(2,1)S(1)} all-to-all(bf16[4,32,1024]{2,0,1:T(4,128)(2,1)S(1)} %copy.131), channel_id=1, replica_groups=mesh['chan'=32,'ctx'=32] {'ctx'}, dimensions={1} | all-to-all | bytes 524288 | tf_op jit(solution)/shard_map/all_to_all | solution.py:69
  271.5 5.6 convert_bitcast_fusion
  277.1 12.0 %copy.136 = bf16[4096,1024]{1,0:T(8,128)(2,1)} copy(bf16[4096,1024]{0,1:T(8,128)(2,1)} %convert_bitcast_fusion) | data formatting | bytes 16777216
  289.1 275.8 %reduce-scatter.4.cloned.1.call-done = bf16[128,1024]{1,0:T(8,128)(2,1)} async-done(((bf16[4096,1024]{1,0:T(8,128)(2,1)}), bf16[128,1024]{1,0:T(8,128)(2,1)}) %reduce-scatter.4.cloned.1.call-update) | async-done | bytes 262160
  564.9 1.8 copy.137
  (112 shorter events, 61.9 us)
Async XLA Ops:
  6.5 264.9 %copy-start = (bf16[128,4096]{1,0:T(8,128)(2,1)S(1)}, bf16[128,4096]{1,0:T(8,128)(2,1)}, u32[]{:S(2)}) copy-start(bf16[128,4096]{1,0:T(8,128)(2,1)} %param.15) | copy-start | bytes 3145732
  6.5 5.4 copy-start.7
  10.0 5.9 %collective-permute-start = (bf16[3,2,128]{1,2,0:T(8,128)(2,1)S(1)}, bf16[3,2,128]{1,2,0:T(8,128)(2,1)S(1)}, u32[]{:S(2)}, u32[]{:S(2)}) collective-permute-start(bf16[3,2,128]{1,2,0:T(8,128)(2,1)S(1)} %pad_maximum_fusion), channel_id=1, source_target_pairs={{0,1},{1,2},{2,3},{3,4},{4,5},{5,6},{6,7},{7,8},{8,9},{9,10},{10,1... | collective-permute-start | bytes 4616 | tf_op jit(solution)/shard_map/ppermute | solution.py:10
  17.6 45.7 %copy-start.10 = (f32[128]{0:T(128)S(1)}, f32[128]{0:T(128)}, u32[]{:S(2)}) copy-start(f32[128]{0:T(128)} %param.14) | copy-start | bytes 1540
  17.6 46.3 %copy-start.5 = (f32[16,128]{1,0:T(8,128)S(1)}, f32[16,128]{1,0:T(8,128)}, u32[]{:S(2)}) copy-start(f32[16,128]{1,0:T(8,128)} %param.12) | copy-start | bytes 24580
  17.6 46.5 %copy-start.6 = (f32[16,128]{1,0:T(8,128)S(1)}, f32[16,128]{1,0:T(8,128)}, u32[]{:S(2)}) copy-start(f32[16,128]{1,0:T(8,128)} %param.13) | copy-start | bytes 24580
  18.5 108.7 %all-to-all-start = ((bf16[32,4,1024]{2,1,0:T(4,128)(2,1)}), bf16[32,4,1024]{2,1,0:T(4,128)(2,1)S(1)}, u32[]{:S(2)}, u32[]{:S(2)}) async-start(bf16[32,4,1024]{2,1,0:T(4,128)(2,1)} %all_to_all.20), calls=%async_computation | async-start | bytes 524288 | tf_op jit(solution)/shard_map/all_to_all | solution.py:60
  63.3 501.7 %reduce-scatter.4.cloned.1.call-start = ((), (), s32[]{:S(2)}) async-start(), calls=%async_computation.3 | async-start | bytes 8650752
  64.1 64.9 %copy-start.3 = (f32[16,4]{0,1:T(4,128)}, f32[16,4]{0,1:T(4,128)S(1)}, u32[]{:S(2)}) copy-start(f32[16,4]{0,1:T(4,128)S(1)} %copy.143) | copy-start | bytes 772
  64.3 2.1 copy-start.4
  66.3 0.6 copy-start.9
  129.4 4.0 copy-start.2
  143.8 8.0 %copy-start.1 = (f32[4,16,16]{1,2,0:T(8,128)}, f32[4,16,16]{1,2,0:T(8,128)S(1)}, u32[]{:S(2)}) copy-start(f32[4,16,16]{1,2,0:T(8,128)S(1)} %multiply_add_fusion.3) | copy-start | bytes 12292
  157.9 47.5 %slice-start = ((f32[4,256,16]{1,2,0:T(8,128)}), f32[4,1,16]{1,2,0:T(8,128)S(1)}, s32[]{:S(2)}) async-start(f32[4,256,16]{1,2,0:T(8,128)} %copy-done.2), calls=%async_computation.4 | async-start | bytes 65536 | tf_op jit(solution)/shard_map/slice | solution.py:39
  209.2 3.1 copy-start.8
Sparse Core Ops, SparseCore 0:
  289.2 275.6 reduce-scatter.3
where the time goes:
time: 577 us; the launch traced here: 574 us
  waiting for transfers between devices  280 us (49%)
  local copies, waits for them, and re-layouts  138 us (24%)
  blocking collectives  55.6 us (10%)
  starting transfers between devices  46.7 us (8%)
  other arithmetic  31.3 us (5%)
  between operations  13.8 us (2%)
  matrix products  8.17 us (1%)
    unnamed x2, waiting for transfers between devices  276 us
    gather x2, local copies, waits for them, and re-layouts, modal_conv(): kernel[:, jnp.clip(lag_index, 0, tile_rows - 1)]  60 us
    all_to_all x1, blocking collectives, local(): lax.all_to_all(answer, 'ctx', split_axis=1, concat_axis=0, tiled=True)  55.6 us
    all_to_all x1, starting transfers between devices, local(): lax.all_to_all(product.T, 'ctx', split_axis=0, concat_axis=1, tiled=True)  44.7 us
    pad x12, local copies, waits for them, and re-layouts, modal_conv(): _, ending = lax.associative_scan(combine, (factor, deposit), axis=1)  30.3 us
    slice x24, local copies, waits for them, and re-layouts, modal_conv(): _, ending = lax.associative_scan(combine, (factor, deposit), axis=1)  20.5 us
    unnamed x32, local copies, waits for them, and re-layouts  20.3 us
    add x14, other arithmetic, combine(): return (first[0] * second[0], first[1] * second[0] + second[1])  12.3 us
  transfers between devices with their start and end apart: 3, of which 2 were waited for; matrix products, arithmetic and copies ran while one was open for 11% of the time, Pallas kernels for 0%

commit v1 on v0

v1 whole, which is shorter than its diff:
```python
from functools import partial

import jax
import jax.numpy as jnp
from jax import lax
from jax.experimental import pallas as pl
from jax.experimental.pallas import tpu as pltpu
from jax.sharding import Mesh, PartitionSpec as P


CTX = ("w", "x", "core")
CHUNKS = 8


def features(padded, ref, tail, taps):
    rows = ref.shape[0]
    padded[6:8, :] = tail.astype(jnp.float32)
    padded[8:, :] = ref[...].astype(jnp.float32)
    total = taps[0:1, :] * padded[8 : 8 + rows, :]
    total = total + taps[1:2, :] * padded[7 : 7 + rows, :]
    return total + taps[2:3, :] * padded[6 : 6 + rows, :]


def first_pass(q, k, v, tail, taps, rates, featq, product, prefix, message, padded, signal):
    rows, chans = q.shape
    length = rows // CHUNKS
    modes = rates.shape[0]
    weights = taps[...].astype(jnp.float32)
    featq[...] = features(padded, q, tail[0], weights[0])
    last_query = padded[rows + 6 :, :]
    keyed = features(padded, k, tail[1], weights[1])
    last_key = padded[rows + 6 :, :]
    valued = features(padded, v, tail[2], weights[2])
    last_value = padded[rows + 6 :, :]
    edges = [keyed[0:2, :], valued[0:2, :], last_key, last_value, last_query]
    edges.append(jnp.zeros((6, chans), jnp.float32))
    prod = (keyed * valued).astype(jnp.bfloat16).astype(jnp.float32)
    product[...] = prod
    signal[...] = prod
    decay = [
        jnp.broadcast_to(jnp.exp(-rates[m : m + 1, :]), (CHUNKS, chans)) for m in range(modes)
    ]

    def step(t, held):
        row = signal[pl.ds(t, CHUNKS, stride=length), :]
        return tuple(decay[m] * held[m] + row for m in range(modes))

    zero = jnp.zeros((CHUNKS, chans), jnp.float32)
    held = lax.fori_loop(0, length, step, (zero,) * modes, unroll=4)
    index = lax.broadcasted_iota(jnp.int32, (CHUNKS, chans), 0)
    left = []
    for m in range(modes):
        rate = rates[m : m + 1, :]
        run = held[m]
        reach = 1
        while reach < CHUNKS:
            before = jnp.where(index >= reach, pltpu.roll(run, reach, 0), 0.0)
            run = run + jnp.exp(-rate * float(length * reach)) * before
            reach *= 2
        prefix[m] = jnp.where(index >= 1, pltpu.roll(run, 1, 0), 0.0)
        left.append(run[CHUNKS - 1 :, :])
    message[...] = jnp.concatenate(left + edges, axis=0)


def joined(rates, own, *rest, axis, span):
    *others, out, before = rest
    values = [own[...]] + [o[...] for o in others]
    modes = rates.shape[0]
    count = len(values)
    here = lax.axis_index(axis)
    decay = jnp.exp(-rates[...] * float(span))
    total = ahead = jnp.zeros(rates.shape, jnp.float32)
    ends = []
    for i in range(count):
        value = values[0]
        for d in range(1, count):
            value = jnp.where(lax.rem(here - d + count, count) == i, values[d], value)
        ends.append(value)
        ahead = jnp.where(i < here, decay * ahead + value[0:modes, :], ahead)
        total = decay * total + value[0:modes, :]
    row = lax.broadcasted_iota(jnp.int32, own.shape, 0)
    edges = jnp.where(row < modes + 4, ends[0], ends[-1])
    out[...] = jnp.concatenate([total, edges[modes:, :]], axis=0)
    before[...] = ahead


def edge_change(message, before, taps, modes):
    def pair(head, tail, weights):
        old0 = message[modes + head : modes + head + 1, :]
        old1 = message[modes + head + 1 : modes + head + 2, :]
        back2 = before[modes + tail : modes + tail + 1, :]
        back1 = before[modes + tail + 1 : modes + tail + 2, :]
        new0 = (old0 + weights[1:2, :] * back1) + weights[2:3, :] * back2
        return old0, old1, new0, old1 + weights[2:3, :] * back1

    def rounded(value):
        return value.astype(jnp.bfloat16).astype(jnp.float32)

    k0, k1, kn0, kn1 = pair(0, 4, taps[1])
    v0, v1, vn0, vn1 = pair(2, 6, taps[2])
    return rounded(kn0 * vn0) - rounded(k0 * v0), rounded(kn1 * vn1) - rounded(k1 * v1)


def second_pass(
    featq, product, prefix, low, mid, own, back1, back2, back3,
    taps, rates, residue, gain, gated, signal, mixed,
):
    rows, chans = product.shape
    length = rows // CHUNKS
    modes = rates.shape[0]
    ncore, nx = lax.axis_size("core"), lax.axis_size("x")
    run = rows * ncore * nx
    core, x = lax.axis_index("core"), lax.axis_index("x")
    rate = rates[...]
    weights = taps[...].astype(jnp.float32)

    def power(tokens):
        return jnp.exp(-rate * tokens)

    chain = [own[...], back1[...], back2[...], back3[...], jnp.zeros(own.shape, jnp.float32)]
    start = jnp.zeros((modes, chans), jnp.float32)
    whole = power(float(run))
    for d in (3, 2, 1):
        first, second = edge_change(chain[d], chain[d + 1], weights, modes)
        total = chain[d][0:modes, :] + power(run - 1.0) * first + power(run - 2.0) * second
        start = whole * start + total
    first, second = edge_change(chain[0], chain[1], weights, modes)
    lost = jnp.exp(rate) * first + jnp.exp(2.0 * rate) * second
    ahead = (x * ncore + core).astype(jnp.float32) * float(rows)
    leads = ahead < 1.0
    back_core = power(core.astype(jnp.float32) * float(rows))
    carried = low[...] + back_core * mid[...] + power(ahead) * (start + jnp.where(leads, 0.0, lost))
    lost = jnp.where(leads, lost, 0.0)

    wide = (CHUNKS, chans)
    row = lax.broadcasted_iota(jnp.int32, wide, 0)
    index = row.astype(jnp.float32)
    dp0, dp1 = jnp.where(leads, first, 0.0), jnp.where(leads, second, 0.0)
    signal[...] = product[...]
    signal[0:CHUNKS, :] = product[0:CHUNKS, :] + jnp.where(
        row == 0, dp0, jnp.where(row == 1, dp1, 0.0)
    )
    held = []
    decay = []
    weight = []
    for m in range(modes):
        one = rate[m : m + 1, :]
        decay.append(jnp.broadcast_to(jnp.exp(-one), wide))
        weight.append(jnp.broadcast_to(residue[m : m + 1, :], wide))
        reach = jnp.exp(-one * (index * float(length)))
        before = carried[m : m + 1, :] + jnp.where(row >= 1, lost[m : m + 1, :], 0.0)
        held.append(prefix[m] + reach * before)

    def step(t, held):
        now = signal[pl.ds(t, CHUNKS, stride=length), :]
        held = tuple(decay[m] * held[m] + now for m in range(modes))
        terms = [weight[m] * held[m] for m in range(modes)]
        while len(terms) > 1:
            terms = [terms[i] + terms[i + 1] for i in range(0, len(terms), 2)]
        mixed[pl.ds(t, CHUNKS, stride=length), :] = terms[0]
        return held

    lax.fori_loop(0, length, step, tuple(held), unroll=2)
    long_out = (mixed[...] + gain[...] * signal[...]).astype(jnp.bfloat16).astype(jnp.float32)
    gated[...] = (featq[...] * long_out).astype(jnp.bfloat16)
    last2 = back1[modes + 8 : modes + 9, :]
    last1 = back1[modes + 9 : modes + 10, :]
    top = lax.broadcasted_iota(jnp.int32, (16, chans), 0)
    dq0 = jnp.where(leads, weights[0][1:2, :] * last1 + weights[0][2:3, :] * last2, 0.0)
    dq1 = jnp.where(leads, weights[0][2:3, :] * last1, 0.0)
    query = featq[0:16, :] + jnp.where(top == 0, dq0, jnp.where(top == 1, dq1, 0.0))
    gated[0:16, :] = (query * long_out[0:16, :]).astype(jnp.bfloat16)


def project(gathered, weights, shares):
    ny, nb = gathered.shape[:2]
    ncore, nx = weights.shape[:2]
    left = jnp.concatenate(
        [gathered[i, j] for i in range(ny) for j in range(nb)], axis=1
    )
    width = shares.shape[2]
    for n in range(0, shares.shape[0], 2):
        cols = slice(n * width, (n + 2) * width)
        right = jnp.concatenate(
            [
                weights[core, x, i, j, :, cols]
                for i in range(ny)
                for j in range(nb)
                for x in range(nx)
                for core in range(ncore)
            ],
            axis=0,
        )
        both = jnp.dot(left, right, preferred_element_type=jnp.float32).astype(shares.dtype)
        shares[n] = both[:, :width]
        shares[n + 1] = both[:, width:]


def moved(value, axis, pairs):
    return lax.ppermute(value, axis, pairs)


def everyone(value, axis):
    count = lax.axis_size(axis)
    return lax.all_to_all(
        jnp.broadcast_to(value[None], (count,) + value.shape), axis, 0, 0, tiled=True
    )


def own_weights(out_weight):
    ny, nb = lax.axis_size("y"), lax.axis_size("zb")
    ncore = lax.axis_size("core")
    share = out_weight.shape[0] // (lax.axis_size("x") * ncore)
    first = (lax.axis_index("x") * ncore + lax.axis_index("core")) * share
    rows = lax.dynamic_slice_in_dim(out_weight, first, share, 0)
    blocks = rows.reshape(share, ny, -1).transpose(1, 0, 2)
    blocks = jnp.broadcast_to(blocks[:, None], (ny, nb) + blocks.shape[1:])
    blocks = blocks.reshape((ny * nb,) + blocks.shape[2:])
    got = lax.all_to_all(blocks, ("y", "zb"), 0, 0, tiled=True)
    return got.reshape((ny, nb) + got.shape[1:])


def layer(
    key_proj, value_proj, query_proj, short_filter, decay_rate, residue, skip_gain, out_weight
):
    rows, chans = key_proj.shape
    modes = decay_rate.shape[0]
    na, nb = lax.axis_size("za"), lax.axis_size("zb")
    ncore, nx, nw = (lax.axis_size(a) for a in ("core", "x", "w"))
    f32 = jnp.float32
    weights = own_weights(out_weight)
    tails = jnp.stack([query_proj[rows - 2 :], key_proj[rows - 2 :], value_proj[rows - 2 :]], 0)
    near = [(i, i + 1) for i in range(nw * nx * ncore - 1) if (i + 1) % (nx * ncore) > 0]
    tails = moved(tails, CTX, near)
    featq, product, prefix, message = pl.pallas_call(
        first_pass,
        out_shape=(
            jax.ShapeDtypeStruct((rows, chans), f32),
            jax.ShapeDtypeStruct((rows, chans), f32),
            jax.ShapeDtypeStruct((modes, CHUNKS, chans), f32),
            jax.ShapeDtypeStruct((modes + 16, chans), f32),
        ),
        scratch_shapes=[pltpu.VMEM((rows + 8, chans), f32), pltpu.VMEM((rows, chans), f32)],
        name="first_pass",
    )(query_proj, key_proj, value_proj, tails, short_filter, decay_rate)

    def join(value, axis, span):
        count = lax.axis_size(axis)
        rest = [
            moved(value, axis, [(i, (i + d) % count) for i in range(count)])
            for d in range(1, count)
        ]
        return pl.pallas_call(
            partial(joined, axis=axis, span=span),
            out_shape=(
                jax.ShapeDtypeStruct((modes + 16, chans), f32),
                jax.ShapeDtypeStruct((modes, chans), f32),
            ),
        )(decay_rate, value, *rest)

    message, low = join(message, "core", rows)
    own, mid = join(message, "x", rows * ncore)
    weights, own = lax.optimization_barrier((weights, own))
    weights = everyone(weights, "x")
    back = {}
    for d in (2, 1, 3):
        back[d] = moved(own, "w", [(i, i + d) for i in range(nw - d)])
    gated = pl.pallas_call(
        second_pass,
        out_shape=jax.ShapeDtypeStruct((rows, chans), jnp.bfloat16),
        scratch_shapes=[pltpu.VMEM((rows, chans), f32), pltpu.VMEM((rows, chans), f32)],
        name="second_pass",
    )(
        featq, product, prefix, low, mid, own, back[1], back[2], back[3],
        short_filter, decay_rate, residue, skip_gain[None],
    )
    weights = everyone(weights, "core")
    quarter = rows // nb
    mine = lax.all_to_all(gated.reshape(nb, quarter, chans), "zb", 0, 0, tiled=True)
    gathered = everyone(mine, "y")
    shares = pl.pallas_call(
        project,
        out_shape=jax.ShapeDtypeStruct((na * nb, quarter, chans), jnp.bfloat16),
        name="project",
    )(gathered, weights)
    parts = lax.all_to_all(shares, ("za", "zb"), 0, 0, tiled=True)
    total = parts.reshape(na, rows, chans).astype(f32).sum(0)
    return total.astype(jnp.bfloat16)


def solution(mesh):
    fine = Mesh(mesh.devices.reshape(4, 2, 4, 4, 4, 2), ("y", "za", "zb") + CTX)
    chan = ("y", "za", "zb")
    placed = (
        P(CTX, chan),
        P(CTX, chan),
        P(CTX, chan),
        P(None, None, chan),
        P(None, chan),
        P(None, chan),
        P(chan),
        P(chan, None),
    )
    return jax.shard_map(layer, mesh=fine, in_specs=placed, out_specs=P(CTX, chan), check_vma=False)
```

time: 577 us -> 168 us (0.29)
  waiting for transfers between devices: 280 us -> 8.17 us
  local copies, waits for them, and re-layouts: 138 us -> 8.51 us
  other arithmetic: 31.3 us -> 0.79 us
  blocking collectives: 55.6 us -> 72.5 us
  Pallas kernels: 0 us -> 15.4 us
  starting transfers between devices: 46.7 us -> 62 us
  between operations: 13.8 us -> 0.18 us
  matrix products: 8.17 us -> 0 us
    unnamed x2 -> x0, waiting for transfers between devices: 276 us -> none
    gather x2 -> x0, local copies, waits for them, and re-layouts: 60 us -> none  [modal_conv(): kernel[:, jnp.clip(lag_index, 0, tile_rows - 1)]]
    ppermute x1 -> x8, starting transfers between devices: 1.92 us -> 47.3 us  [moved(): return lax.ppermute(value, axis, pairs)]
    pad x12 -> x0, local copies, waits for them, and re-layouts: 30.3 us -> none  [modal_conv(): _, ending = lax.associative_scan(combine, (factor, deposit), axis=1)]
    all_to_all x1 -> x2, starting transfers between devices: 44.7 us -> 14.7 us  [the longest x1 8.64 us: own_weights(): got = lax.all_to_all(blocks, ('y', 'zb'), 0, 0, tiled=True)]
    slice x26 -> x0, local copies, waits for them, and re-layouts: 21.8 us -> none  [the longest x24 20.5 us: modal_conv(): _, ending = lax.associative_scan(combine, (factor, deposit), axis=1)]
    add x23 -> x0, other arithmetic: 21 us -> none  [the longest x14 12.3 us: combine(): return (first[0] * second[0], first[1] * second[0] + second[1])]
    all_to_all x1 -> x4, blocking collectives: 55.6 us -> 72.5 us  [the longest x1 33.1 us: layer(): parts = lax.all_to_all(shares, ('za', 'zb'), 0, 0, tiled=True)]
  transfers between devices with their start and end apart: 3 -> 10, of which waited for: 2 -> 5; matrix products, arithmetic and copies ran while one was open for 11% -> 1% of each run, Pallas kernels for 0% -> 6%
where the time goes in v1:
time: 168 us
  blocking collectives  72.5 us (43%)
  starting transfers between devices  62 us (37%)
  Pallas kernels  15.4 us (9%)
  local copies, waits for them, and re-layouts  8.51 us (5%)
  waiting for transfers between devices  8.17 us (5%)
    ppermute x8, starting transfers between devices, moved(): return lax.ppermute(value, axis, pairs)  47.3 us
    all_to_all x1, blocking collectives, layer(): parts = lax.all_to_all(shares, ('za', 'zb'), 0, 0, tiled=True)  33.1 us
    all_to_all x2, blocking collectives, everyone(): lax.all_to_all(jnp.broadcast_to(value[None], (count,) + value.shape), axi...  25.4 us
    all_to_all x1, blocking collectives, layer(): lax.all_to_all(gated.reshape(nb, quarter, chans), 'zb', 0, 0, tiled=True)  14 us
    all_to_all x1, starting transfers between devices, own_weights(): got = lax.all_to_all(blocks, ('y', 'zb'), 0, 0, tiled=True)  8.64 us
    ppermute x8, waiting for transfers between devices, moved(): return lax.ppermute(value, axis, pairs)  8.16 us
    all_to_all x1, starting transfers between devices, everyone(): lax.all_to_all(jnp.broadcast_to(value[None], (count,) + value.shape), axi...  6.08 us
    pallas_call x1, Pallas kernels, layer(): pl.pallas_call(project, out_shape=jax.ShapeDtypeStruct((na * nb, quarter,...  4.56 us
  transfers between devices with their start and end apart: 10, of which 5 were waited for; matrix products, arithmetic and copies ran while one was open for 1% of the time, Pallas kernels for 6%

profile of v1, /device:TPU:2, one launch (start us, length us, event | category | flops | bytes accessed | tf_op | source)
XLA Modules:
  0.0 167.5 jit_solution(18170836403609294991)
XLA Ops:
  2.2 8.6 %all-to-all-start = ((bf16[16,16,1024]{2,1,0:T(8,128)(2,1)}), bf16[16,16,1024]{2,1,0:T(8,128)(2,1)S(1)}, u32[]{:S(2)}, u32[]{:S(2)}) async-start(bf16[16,16,1024]{2,1,0:T(8,128)(2,1)} %bitcast.4), calls=%async_computation | async-start | bytes 1048576 | tf_op jit(solution)/shard_map/all_to_all | solution.py:219
  12.3 1.9 %collective-permute-start = (bf16[3,2,128]{2,1,0:T(2,128)(2,1)S(1)}, bf16[3,2,128]{2,1,0:T(2,128)(2,1)S(1)}, u32[]{:S(2)}, u32[]{:S(2)}) collective-permute-start(bf16[3,2,128]{2,1,0:T(2,128)(2,1)S(1)} %pad_maximum_fusion), channel_id=1, source_target_pairs={{0,1},{1,2},{2,3},{3,4},{4,5},{5,6},{6,7},{8,9},{9,10},{10,11},{11... | collective-permute-start | bytes 4616 | tf_op jit(solution)/shard_map/ppermute | solution.py:200
  14.2 3.0 %collective-permute-done.tail = bf16[3,2,128]{2,1,0:T(2,128)(2,1)S(1)} collective-permute-done((bf16[3,2,128]{2,1,0:T(2,128)(2,1)S(1)}, bf16[3,2,128]{2,1,0:T(2,128)(2,1)S(1)}, u32[]{:S(2)}, u32[]{:S(2)}) %collective-permute-start) | collective-permute-done | bytes 1568 | tf_op jit(solution)/shard_map/ppermute | solution.py:200
  17.8 3.8 %first_pass.1 = (f32[1024,128]{1,0:T(8,128)}, f32[1024,128]{1,0:T(8,128)}, f32[16,8,128]{2,1,0:T(8,128)}, f32[32,128]{1,0:T(8,128)}) custom-call(bf16[1024,128]{1,0:T(8,128)(2,1)} %q.1, bf16[1024,128]{1,0:T(8,128)(2,1)} %k.1, bf16[1024,128]{1,0:T(8,128)(2,1)} %v.1, bf16[3,2,128]{2,1,0:T(2,128)(2,1)} %copy-done.10, bf16[3,3,128]{2,1,0:T(4,128)(2,1)} %taps.3, ...), custom_call_target="tpu_custom_call" | custom-call | tf_op jit(solution)/shard_map/first_pass/pallas_call | solution.py:235
  21.6 1.9 %collective-permute-start.1 = (f32[32,128]{1,0:T(8,128)}, f32[32,128]{1,0:T(8,128)S(1)}, u32[]{:S(2)}, u32[]{:S(2)}) collective-permute-start(f32[32,128]{1,0:T(8,128)} %get-tuple-element.18.own), channel_id=1, source_target_pairs={{0,1},{1,0},{2,3},{3,2},{4,5},{5,4},{6,7},{7,6},{8,9},{9,8},{10,11... | collective-permute-start | bytes 49160 | tf_op jit(solution)/shard_map/ppermute | solution.py:200
  23.5 1.4 collective-permute-done.1.rest_0_
  25.4 1.4 shard_map.82
  26.8 7.2 %collective-permute-start.4 = (f32[32,128]{1,0:T(8,128)}, f32[32,128]{1,0:T(8,128)S(1)}, u32[]{:S(2)}, u32[]{:S(2)}) collective-permute-start(f32[32,128]{1,0:T(8,128)} %get-tuple-element.20.own), channel_id=1, source_target_pairs={{0,6},{2,0},{4,2},{6,4},{1,7},{3,1},{5,3},{7,5},{8,14},{10,8},{12,... | collective-permute-start | bytes 49160 | tf_op jit(solution)/shard_map/ppermute | solution.py:200
  34.0 1.9 %collective-permute-start.3 = (f32[32,128]{1,0:T(8,128)}, f32[32,128]{1,0:T(8,128)S(1)}, u32[]{:S(2)}, u32[]{:S(2)}) collective-permute-start(f32[32,128]{1,0:T(8,128)} %get-tuple-element.20.own), channel_id=1, source_target_pairs={{0,4},{2,6},{4,0},{6,2},{1,5},{3,7},{5,1},{7,3},{8,12},{10,14},{12... | collective-permute-start | bytes 49160 | tf_op jit(solution)/shard_map/ppermute | solution.py:200
  35.9 3.4 %collective-permute-start.2 = (f32[32,128]{1,0:T(8,128)}, f32[32,128]{1,0:T(8,128)S(1)}, u32[]{:S(2)}, u32[]{:S(2)}) collective-permute-start(f32[32,128]{1,0:T(8,128)} %get-tuple-element.20.own), channel_id=1, source_target_pairs={{0,2},{2,4},{4,6},{6,0},{1,3},{3,5},{5,7},{7,1},{8,10},{10,12},{12... | collective-permute-start | bytes 49160 | tf_op jit(solution)/shard_map/ppermute | solution.py:200
  39.3 2.0 %collective-permute-done.3.rest_1_ = f32[32,128]{1,0:T(8,128)S(1)} collective-permute-done((f32[32,128]{1,0:T(8,128)}, f32[32,128]{1,0:T(8,128)S(1)}, u32[]{:S(2)}, u32[]{:S(2)}) %collective-permute-start.3) | collective-permute-done | bytes 16416 | tf_op jit(solution)/shard_map/ppermute | solution.py:200
  42.6 1.4 shard_map.83
  44.0 1.6 broadcast_in_dim.13
  45.6 6.1 %all-to-all-start.3 = ((bf16[4,4,4,16,1024]{4,3,2,1,0:T(8,128)(2,1)}), bf16[4,4,4,16,1024]{4,3,2,1,0:T(8,128)(2,1)S(1)}, u32[]{:S(2)}, u32[]{:S(2)}) async-start(bf16[4,4,4,16,1024]{4,3,2,1,0:T(8,128)(2,1)} %broadcast_in_dim.13), calls=%async_computation.3 | async-start | bytes 4194304 | tf_op jit(solution)/shard_map/all_to_all | solution.py:205
  51.7 17.6 %collective-permute-start.7 = (f32[32,128]{1,0:T(8,128)S(1)}, f32[32,128]{1,0:T(8,128)S(1)}, u32[]{:S(2)}, u32[]{:S(2)}) collective-permute-start(f32[32,128]{1,0:T(8,128)S(1)} %copy-done.2), channel_id=1, source_target_pairs={{0,24},{1,25},{2,26},{3,27},{4,28},{5,29},{6,30},{7,31},{32,56},{3... | collective-permute-start | bytes 49160 | tf_op jit(solution)/shard_map/ppermute | solution.py:200
  69.3 6.6 %collective-permute-start.6 = (f32[32,128]{1,0:T(8,128)S(1)}, f32[32,128]{1,0:T(8,128)S(1)}, u32[]{:S(2)}, u32[]{:S(2)}) collective-permute-start(f32[32,128]{1,0:T(8,128)S(1)} %copy-done.2), channel_id=1, source_target_pairs={{0,16},{8,24},{1,17},{9,25},{2,18},{10,26},{3,19},{11,27},{4,20},{... | collective-permute-start | bytes 49160 | tf_op jit(solution)/shard_map/ppermute | solution.py:200
  75.9 6.7 %collective-permute-start.5 = (f32[32,128]{1,0:T(8,128)S(1)}, f32[32,128]{1,0:T(8,128)S(1)}, u32[]{:S(2)}, u32[]{:S(2)}) collective-permute-start(f32[32,128]{1,0:T(8,128)S(1)} %copy-done.2), channel_id=1, source_target_pairs={{0,8},{8,16},{16,24},{1,9},{9,17},{17,25},{2,10},{10,18},{18,26},{... | collective-permute-start | bytes 49160 | tf_op jit(solution)/shard_map/ppermute | solution.py:200
  82.7 1.4 collective-permute-done.5.back1
  84.7 4.2 %second_pass.1 = bf16[1024,128]{1,0:T(8,128)(2,1)} custom-call(f32[1024,128]{1,0:T(8,128)} %get-tuple-element.15.featq, f32[1024,128]{1,0:T(8,128)} %get-tuple-element.16.product, f32[16,8,128]{2,1,0:T(8,128)} %get-tuple-element.17.prefix, f32[16,128]{1,0:T(8,128)} %get-tuple-element.19.low, f32[16,128]{1,0:T(8,128)} %get-tuple-element.21.mid, ...), custom_call_target="tpu_custom_call" | custom-call | tf_op jit(solution)/shard_map/second_pass/pallas_call | solution.py:268
  89.5 8.3 %all_to_all.30.weights = bf16[2,4,4,4,16,1024]{5,4,3,2,1,0:T(8,128)(2,1)} all-to-all(bf16[2,4,4,4,16,1024]{5,4,3,2,1,0:T(8,128)(2,1)S(1)} %broadcast_in_dim.14), channel_id=1, replica_groups=mesh['y'=4,'za'=2,'zb'=4,'w'=4,'x'=4,'core'=2] {'core'}, dimensions={0} | all-to-all | bytes 8388608 | tf_op jit(solution)/shard_map/all_to_all | solution.py:205
  97.8 14.0 %all_to_all.31 = bf16[4,256,128]{2,1,0:T(8,128)(2,1)S(1)} all-to-all(bf16[4,256,128]{2,1,0:T(8,128)(2,1)S(1)} %bitcast.16), channel_id=1, replica_groups=mesh['y'=4,'za'=2,'zb'=4,'w'=4,'x'=4,'core'=2] {'zb'}, dimensions={0} | all-to-all | bytes 524288 | tf_op jit(solution)/shard_map/all_to_all | solution.py:279
  111.9 17.1 %all_to_all.32.gathered = bf16[4,4,256,128]{3,2,1,0:T(8,128)(2,1)} all-to-all(bf16[4,4,256,128]{3,2,1,0:T(8,128)(2,1)S(1)} %broadcast_in_dim.12), channel_id=1, replica_groups=mesh['y'=4,'za'=2,'zb'=4,'w'=4,'x'=4,'core'=2] {'y'}, dimensions={0} | all-to-all | bytes 2097152 | tf_op jit(solution)/shard_map/all_to_all | solution.py:205
  129.1 4.6 %project.1 = bf16[8,256,128]{2,1,0:T(8,128)(2,1)} custom-call(bf16[4,4,256,128]{3,2,1,0:T(8,128)(2,1)} %all_to_all.32.gathered, bf16[2,4,4,4,16,1024]{5,4,3,2,1,0:T(8,128)(2,1)} %all_to_all.30.weights), custom_call_target="tpu_custom_call" | custom-call | tf_op jit(solution)/shard_map/project/pallas_call | solution.py:281
  133.6 33.1 %all_to_all.33 = bf16[8,256,128]{2,1,0:T(8,128)(2,1)S(1)} all-to-all(bf16[8,256,128]{2,1,0:T(8,128)(2,1)} %project.1), channel_id=1, replica_groups=mesh['y'=4,'za'=2,'zb'=4,'w'=4,'x'=4,'core'=2] {'za','zb'}, dimensions={0} | all-to-all | bytes 1048576 | tf_op jit(solution)/shard_map/all_to_all | solution.py:286
  (38 shorter events, 8.1 us)
Async XLA Ops:
  0.0 1.2 copy-start
  2.2 41.7 %all-to-all-start = ((bf16[16,16,1024]{2,1,0:T(8,128)(2,1)}), bf16[16,16,1024]{2,1,0:T(8,128)(2,1)S(1)}, u32[]{:S(2)}, u32[]{:S(2)}) async-start(bf16[16,16,1024]{2,1,0:T(8,128)(2,1)} %bitcast.4), calls=%async_computation | async-start | bytes 1048576 | tf_op jit(solution)/shard_map/all_to_all | solution.py:219
  12.3 4.9 %collective-permute-start = (bf16[3,2,128]{2,1,0:T(2,128)(2,1)S(1)}, bf16[3,2,128]{2,1,0:T(2,128)(2,1)S(1)}, u32[]{:S(2)}, u32[]{:S(2)}) collective-permute-start(bf16[3,2,128]{2,1,0:T(2,128)(2,1)S(1)} %pad_maximum_fusion), channel_id=1, source_target_pairs={{0,1},{1,2},{2,3},{3,4},{4,5},{5,6},{6,7},{8,9},{9,10},{10,11},{11... | collective-permute-start | bytes 4616 | tf_op jit(solution)/shard_map/ppermute | solution.py:200
  17.2 0.6 copy-start.10
  21.6 3.3 %collective-permute-start.1 = (f32[32,128]{1,0:T(8,128)}, f32[32,128]{1,0:T(8,128)S(1)}, u32[]{:S(2)}, u32[]{:S(2)}) collective-permute-start(f32[32,128]{1,0:T(8,128)} %get-tuple-element.18.own), channel_id=1, source_target_pairs={{0,1},{1,0},{2,3},{3,2},{4,5},{5,4},{6,7},{7,6},{8,9},{9,8},{10,11... | collective-permute-start | bytes 49160 | tf_op jit(solution)/shard_map/ppermute | solution.py:200
  24.8 0.6 copy-start.6
  26.8 12.5 %collective-permute-start.4 = (f32[32,128]{1,0:T(8,128)}, f32[32,128]{1,0:T(8,128)S(1)}, u32[]{:S(2)}, u32[]{:S(2)}) collective-permute-start(f32[32,128]{1,0:T(8,128)} %get-tuple-element.20.own), channel_id=1, source_target_pairs={{0,6},{2,0},{4,2},{6,4},{1,7},{3,1},{5,3},{7,5},{8,14},{10,8},{12,... | collective-permute-start | bytes 49160 | tf_op jit(solution)/shard_map/ppermute | solution.py:200
  34.0 7.3 %collective-permute-start.3 = (f32[32,128]{1,0:T(8,128)}, f32[32,128]{1,0:T(8,128)S(1)}, u32[]{:S(2)}, u32[]{:S(2)}) collective-permute-start(f32[32,128]{1,0:T(8,128)} %get-tuple-element.20.own), channel_id=1, source_target_pairs={{0,4},{2,6},{4,0},{6,2},{1,5},{3,7},{5,1},{7,3},{8,12},{10,14},{12... | collective-permute-start | bytes 49160 | tf_op jit(solution)/shard_map/ppermute | solution.py:200
  35.9 5.8 %collective-permute-start.2 = (f32[32,128]{1,0:T(8,128)}, f32[32,128]{1,0:T(8,128)S(1)}, u32[]{:S(2)}, u32[]{:S(2)}) collective-permute-start(f32[32,128]{1,0:T(8,128)} %get-tuple-element.20.own), channel_id=1, source_target_pairs={{0,2},{2,4},{4,6},{6,0},{1,3},{3,5},{5,7},{7,1},{8,10},{10,12},{12... | collective-permute-start | bytes 49160 | tf_op jit(solution)/shard_map/ppermute | solution.py:200
  39.3 2.5 %copy-start.7 = (f32[32,128]{1,0:T(8,128)}, f32[32,128]{1,0:T(8,128)S(1)}, u32[]{:S(2)}) copy-start(f32[32,128]{1,0:T(8,128)S(1)} %collective-permute-done.4.rest_2_) | copy-start | bytes 49156
  41.4 0.6 copy-start.8
  42.0 0.6 copy-start.9
  44.0 7.7 %copy-start.2 = (f32[32,128]{1,0:T(8,128)S(1)}, f32[32,128]{1,0:T(8,128)}, u32[]{:S(2)}) copy-start(f32[32,128]{1,0:T(8,128)} %get-tuple-element.23.own) | copy-start | bytes 49156
  45.6 43.3 %all-to-all-start.3 = ((bf16[4,4,4,16,1024]{4,3,2,1,0:T(8,128)(2,1)}), bf16[4,4,4,16,1024]{4,3,2,1,0:T(8,128)(2,1)S(1)}, u32[]{:S(2)}, u32[]{:S(2)}) async-start(bf16[4,4,4,16,1024]{4,3,2,1,0:T(8,128)(2,1)} %broadcast_in_dim.13), calls=%async_computation.3 | async-start | bytes 4194304 | tf_op jit(solution)/shard_map/all_to_all | solution.py:205
  51.7 31.0 %collective-permute-start.7 = (f32[32,128]{1,0:T(8,128)S(1)}, f32[32,128]{1,0:T(8,128)S(1)}, u32[]{:S(2)}, u32[]{:S(2)}) collective-permute-start(f32[32,128]{1,0:T(8,128)S(1)} %copy-done.2), channel_id=1, source_target_pairs={{0,24},{1,25},{2,26},{3,27},{4,28},{5,29},{6,30},{7,31},{32,56},{3... | collective-permute-start | bytes 49160 | tf_op jit(solution)/shard_map/ppermute | solution.py:200
  69.3 13.4 %collective-permute-start.6 = (f32[32,128]{1,0:T(8,128)S(1)}, f32[32,128]{1,0:T(8,128)S(1)}, u32[]{:S(2)}, u32[]{:S(2)}) collective-permute-start(f32[32,128]{1,0:T(8,128)S(1)} %copy-done.2), channel_id=1, source_target_pairs={{0,16},{8,24},{1,17},{9,25},{2,18},{10,26},{3,19},{11,27},{4,20},{... | collective-permute-start | bytes 49160 | tf_op jit(solution)/shard_map/ppermute | solution.py:200
  75.9 8.2 %collective-permute-start.5 = (f32[32,128]{1,0:T(8,128)S(1)}, f32[32,128]{1,0:T(8,128)S(1)}, u32[]{:S(2)}, u32[]{:S(2)}) collective-permute-start(f32[32,128]{1,0:T(8,128)S(1)} %copy-done.2), channel_id=1, source_target_pairs={{0,8},{8,16},{16,24},{1,9},{9,17},{17,25},{2,10},{10,18},{18,26},{... | collective-permute-start | bytes 49160 | tf_op jit(solution)/shard_map/ppermute | solution.py:200
  82.7 1.4 copy-start.3
  82.7 1.4 copy-start.4
  84.1 0.6 copy-start.5
  89.5 8.3 %copy-start.1 = (bf16[1024,128]{1,0:T(8,128)(2,1)S(1)}, bf16[1024,128]{1,0:T(8,128)(2,1)}, u32[]{:S(2)}) copy-start(bf16[1024,128]{1,0:T(8,128)(2,1)} %second_pass.1) | copy-start | bytes 786436
